TPU v7x, 512 devices: a whole 4x4x16 slice. The times are simulated.
512 devices in a mesh: frame: 64 (over x, z_lo, core), head: 8 (over z_hi, y).
Axes of the slice: x: 4, y: 4, z: 16 (z_hi: 2, z_lo: 8; z = z_hi * 8 + z_lo), core: 2. Of those that a mesh axis runs over, the one named last changes fastest.
Arguments:
- queries: bfloat16 [65536, 1024], P(('frame', 'head')), may hold values from -8 to 8
- key_vectors: bfloat16 [65536, 1024], P(('frame', 'head')), may hold values from -5 to 5
- value_vectors: bfloat16 [65536, 1024], P(('frame', 'head')), may hold values from -6 to 6
- tile_lists: int32 [8, 512, 20], P('head', 'frame'), may hold values from 0 to 511, as said below
- live_slots: int32 [8, 512], P('head', 'frame'), may hold values from 2 to 20
Outputs:
- attended: bfloat16 [65536, 1024], P(('frame', 'head'))
Inputs may be any that keep to these rules, and one draw needn't show every extreme that they name: `tile_lists`: slot 0 of query tile t holds t; the slots below live_slots hold distinct tiles u with |u - t| <= 32; the other slots hold t.
All inputs are finite; a program needn't handle non-finite values.
Results may differ from a plain program's by a relative error of at most 0.0045.
Values may be sent and summed in bfloat16 or wider, within the bound.
A program may use at most 64 MiB of HBM per device.

v0:
```python
import math

import jax
import jax.numpy as jnp
from jax import lax
from jax.sharding import PartitionSpec as P

TILE = 128
HEAD_DIM = 128
FRAME_TILES = 28
JITTER = 4


def shifted(block, axis, distance):
    devices = range(lax.axis_size(axis))
    route = [(i - distance, i) for i in devices if i - distance in devices]
    return lax.ppermute(block, axis, route)


def masked_softmax(query_tile_rows, gathered_key_block, gathered_value_block, usable):
    softmax_scale = 1.0 / math.sqrt(query_tile_rows.shape[-1])
    logit_scores = (
        jnp.einsum(
            "mar,mxr->max", query_tile_rows, gathered_key_block, preferred_element_type=jnp.float32
        )
        * softmax_scale
    )
    logit_scores = jnp.where(usable[:, None, :], logit_scores, -jnp.inf)
    highest = jnp.max(logit_scores, axis=-1, keepdims=True)
    exponent = jnp.exp(logit_scores - highest)
    denominator = jnp.sum(exponent, axis=-1, keepdims=True)
    weighted_sum = jnp.einsum(
        "fve,fez->fvz",
        exponent.astype(jnp.bfloat16),
        gathered_value_block,
        preferred_element_type=jnp.float32,
    )
    return (weighted_sum / denominator).astype(jnp.bfloat16)


def body(queries, key_vectors, value_vectors, tile_lists, live_slots):
    query_head, key_head, value_head = (
        lax.all_to_all(queries, "head", split_axis=1, concat_axis=0, tiled=True),
        lax.all_to_all(key_vectors, "head", split_axis=1, concat_axis=0, tiled=True),
        lax.all_to_all(value_vectors, "head", split_axis=1, concat_axis=0, tiled=True),
    )
    rows_here = query_head.shape[0]
    tiles_here = rows_here // TILE
    shards = -(-(FRAME_TILES + JITTER) // tiles_here)
    paired = jnp.stack((key_head, value_head))
    lower_pieces = []
    upper_pieces = []
    for distance in range(1, shards + 1):
        lower_pieces.append(shifted(paired, "frame", distance))
        upper_pieces.append(shifted(paired, "frame", -distance))
    window = jnp.concatenate(lower_pieces[::-1] + [paired] + upper_pieces, axis=1)
    window_tiles = window.shape[1] // TILE
    first_tile = (lax.axis_index("frame") - shards) * tiles_here
    block_tiles = min(tiles_here, max(1, 512 // TILE))
    block_count = tiles_here // block_tiles
    key_tiles = window[0].reshape(window_tiles, TILE, HEAD_DIM)
    value_tiles = window[1].reshape(window_tiles, TILE, HEAD_DIM)
    query_tile_rows = query_head.reshape(block_count, block_tiles, TILE, HEAD_DIM)
    local_ids = (tile_lists[0] - first_tile).reshape(block_count, block_tiles, -1)
    living = live_slots[0].reshape(block_count, block_tiles)

    def one_block(pieces, key_tiles=key_tiles, value_tiles=value_tiles):
        block_queries, block_ids, block_live = pieces
        slot_count = block_ids.shape[1]
        gathered_key_block = key_tiles[block_ids].reshape(block_tiles, slot_count * TILE, HEAD_DIM)
        gathered_value_block = value_tiles[block_ids].reshape(
            block_tiles, slot_count * TILE, HEAD_DIM
        )
        slot_ids = jnp.arange(slot_count, dtype=jnp.int32)
        usable = jnp.repeat(slot_ids[None, :] < block_live[:, None], TILE, axis=1)
        attended_block = masked_softmax(
            block_queries, gathered_key_block, gathered_value_block, usable
        )
        return attended_block

    result = lax.map(one_block, (query_tile_rows, local_ids, living))
    outputs = result.reshape(rows_here, HEAD_DIM)
    return lax.all_to_all(outputs, "head", split_axis=0, concat_axis=1, tiled=True)


def solution(mesh):
    placed = (
        P(("frame", "head"), None),
        P(("frame", "head"), None),
        P(("frame", "head"), None),
        P("head", "frame", None),
        P("head", "frame"),
    )
    return jax.shard_map(
        body, mesh=mesh, in_specs=placed, out_specs=P(("frame", "head"), None), check_vma=False
    )
```

profile of v0, /device:TPU:36, one launch (start us, length us, event | category | flops | bytes accessed | tf_op | source)
XLA Modules:
  0.0 243.4 jit_solution(10367581617345590051)
XLA Ops:
  0.0 1.2 copy.16
  1.2 0.9 copy.17
  2.0 16.8 %all-to-all-start.1 = ((bf16[128,8,128]{2,0,1:T(8,128)(2,1)}), bf16[128,8,128]{2,0,1:T(8,128)(2,1)S(1)}, u32[]{:S(2)}, u32[]{:S(2)}) async-start(bf16[128,8,128]{2,0,1:T(8,128)(2,1)} %copy.17), calls=%async_computation.1 | async-start | bytes 524288 | tf_op jit(solution)/shard_map/all_to_all | solution.py:44
  18.9 1.1 copy.18
  20.0 0.2 copy.19
  20.2 23.0 %all-to-all-done.1 = bf16[128,8,128]{2,0,1:T(8,128)(2,1)S(1)} async-done(((bf16[128,8,128]{2,0,1:T(8,128)(2,1)}), bf16[128,8,128]{2,0,1:T(8,128)(2,1)S(1)}, u32[]{:S(2)}, u32[]{:S(2)}) %all-to-all-start.1) | async-done | bytes 262176 | tf_op jit(solution)/shard_map/all_to_all | solution.py:44
  43.2 20.1 %all_to_all.67 = bf16[128,8,128]{2,0,1:T(8,128)(2,1)S(1)} all-to-all(bf16[128,8,128]{2,0,1:T(8,128)(2,1)S(1)} %copy.19), channel_id=1, replica_groups=mesh['frame'=64,'head'=8] {'head'}, dimensions={1} | all-to-all | bytes 524288 | tf_op jit(solution)/shard_map/all_to_all | solution.py:45
  63.4 1.9 collective-permute-start
  65.3 1.9 collective-permute-start.1
  67.2 1.9 collective-permute-start.2
  69.2 0.8 copy_bitcast_fusion.1
  69.9 3.4 %all-to-all-start = ((bf16[128,8,128]{2,0,1:T(8,128)(2,1)}), bf16[128,8,128]{2,0,1:T(8,128)(2,1)S(1)}, u32[]{:S(2)}, u32[]{:S(2)}) async-start(bf16[128,8,128]{2,0,1:T(8,128)(2,1)} %copy_bitcast_fusion.1), calls=%async_computation | async-start | bytes 524288 | tf_op jit(solution)/shard_map/all_to_all | solution.py:43
  73.3 0.5 broadcast.40
  73.9 0.7 reduce.3
  74.5 0.1 reshape_squeeze.9
  74.6 5.6 %collective-permute-start.3 = (bf16[2,1024,128]{2,1,0:T(8,128)(2,1)S(1)}, bf16[2,1024,128]{2,1,0:T(8,128)(2,1)S(1)}, u32[]{:S(2)}, u32[]{:S(2)}) collective-permute-start(bf16[2,1024,128]{2,1,0:T(8,128)(2,1)S(1)} %pad_maximum_fusion), channel_id=1, source_target_pairs={{0,8},{8,16},{16,24},{24,32},{32,40},{40,48},{48,56},{56,64},{64,7... | collective-permute-start | bytes 1572872 | tf_op jit(solution)/shard_map/ppermute | solution.py:17
  80.3 1.9 collective-permute-start.4
  82.2 6.2 %collective-permute-done = bf16[2,1024,128]{2,1,0:T(8,128)(2,1)S(1)} collective-permute-done((bf16[2,1024,128]{2,1,0:T(8,128)(2,1)S(1)}, bf16[2,1024,128]{2,1,0:T(8,128)(2,1)S(1)}, u32[]{:S(2)}, u32[]{:S(2)}) %collective-permute-start) | collective-permute-done | bytes 524320 | tf_op jit(solution)/shard_map/ppermute | solution.py:17
  88.4 41.6 %collective-permute-start.5 = (bf16[2,1024,128]{2,1,0:T(8,128)(2,1)S(1)}, bf16[2,1024,128]{2,1,0:T(8,128)(2,1)S(1)}, u32[]{:S(2)}, u32[]{:S(2)}) collective-permute-start(bf16[2,1024,128]{2,1,0:T(8,128)(2,1)S(1)} %pad_maximum_fusion), channel_id=1, source_target_pairs={{16,0},{24,8},{32,16},{40,24},{48,32},{56,40},{64,48},{72,56},{80,... | collective-permute-start | bytes 1572872 | tf_op jit(solution)/shard_map/ppermute | solution.py:17
  130.1 1.9 collective-permute-start.6
  132.1 1.9 collective-permute-start.7
  134.1 0.1 constant_dynamic-update-slice_fusion.5
  134.4 24.0 %collective-permute-done.5 = bf16[2,1024,128]{2,1,0:T(8,128)(2,1)S(1)} collective-permute-done((bf16[2,1024,128]{2,1,0:T(8,128)(2,1)S(1)}, bf16[2,1024,128]{2,1,0:T(8,128)(2,1)S(1)}, u32[]{:S(2)}, u32[]{:S(2)}) %collective-permute-start.5) | collective-permute-done | bytes 524320 | tf_op jit(solution)/shard_map/ppermute | solution.py:17
  158.5 16.6 %collective-permute-done.6 = bf16[2,1024,128]{2,1,0:T(8,128)(2,1)S(1)} collective-permute-done((bf16[2,1024,128]{2,1,0:T(8,128)(2,1)S(1)}, bf16[2,1024,128]{2,1,0:T(8,128)(2,1)S(1)}, u32[]{:S(2)}, u32[]{:S(2)}) %collective-permute-start.6) | collective-permute-done | bytes 524320 | tf_op jit(solution)/shard_map/ppermute | solution.py:17
  175.2 6.6 %collective-permute-done.7 = bf16[2,1024,128]{2,1,0:T(8,128)(2,1)S(1)} collective-permute-done((bf16[2,1024,128]{2,1,0:T(8,128)(2,1)S(1)}, bf16[2,1024,128]{2,1,0:T(8,128)(2,1)S(1)}, u32[]{:S(2)}, u32[]{:S(2)}) %collective-permute-start.7) | collective-permute-done | bytes 524320 | tf_op jit(solution)/shard_map/ppermute | solution.py:17
  181.9 2.3 fusion.22
  184.2 26.8 %while.10 = (s32[]{:T(128)}, bf16[2,4,128,128]{3,2,1,0:T(8,128)(2,1)S(1)}, s32[2,4]{1,0:T(2,128)S(1)}, bf16[2,4,128,128]{3,2,1,0:T(8,128)(2,1)S(1)}, s32[2,4,20]...) while((s32[]{:T(128)}, ...), condition=%wide.region_3.4_spmd, body=%wide.region_0.3_spmd.sunk | while | flops 680395072 | bytes 52748816 | solution.py:81
  184.2 0.1 reshape.103
  184.3 2.7 %gather_fusion.1 = bf16[80,128,128]{2,1,0:T(8,128)(2,1)S(1)} fusion(bf16[72,128,128]{2,1,0:T(8,128)(2,1)} %get-tuple-element.129, s32[1024]{0:T(1024)S(1)} %pad_clamp_fusion.2), kind=kCustom, calls=%fused_computation.clone.1 | custom fusion | bytes 5243200 | tf_op jit(solution)/shard_map/while/body/eval_jaxpr/gather | solution.py:70
  187.1 0.1 iota_compare_fusion.2
  187.1 0.1 broadcast_bitcast_fusion.2
  187.2 0.9 fusion.37
  188.2 2.3 copy-done.1
  190.5 0.8 fusion.38
  191.3 2.7 %gather_fusion = bf16[80,128,128]{2,1,0:T(8,128)(2,1)S(1)} fusion(bf16[72,128,128]{2,1,0:T(8,128)(2,1)} %get-tuple-element.130, s32[1024]{0:T(1024)S(1)} %pad_clamp_fusion.2), kind=kCustom, calls=%fused_computation.1.clone.1 | custom fusion | bytes 5243200 | tf_op jit(solution)/shard_map/while/body/eval_jaxpr/gather | solution.py:71
  194.0 3.5 %fusion.39 = bf16[2,4,128,128]{3,2,1,0:T(8,128)(2,1)S(1)} fusion(bf16[2,4,128,128]{3,2,1,0:T(8,128)(2,1)S(1)} %get-tuple-element.117, s32[]{:T(128)} %get-tuple-element.116, bf16[4,2560,128]{2,1,0:T(8,128)(2,1)S(1)} %bitcast.67, f32[4,128,2560]{2,1,0:T(8,128)} %copy-done.1, f32[4,128]{1,0:T(4,128)S(1)} %get-tuple-element.107, f32[4,128]{1,0:T(4,128)S(1)} %fusion.38), kind=kOutput, calls=%fused_computation.11.clone.1 | convolution fusion | flops 338296832 | bytes 7999492 | tf_op jit(solution)/shard_map/while/body/eval_jaxpr/fve,fez->fvz/dot_general | solution.py:32
  197.6 0.1 reshape.103
  197.7 2.7 %gather_fusion.1 = bf16[80,128,128]{2,1,0:T(8,128)(2,1)S(1)} fusion(bf16[72,128,128]{2,1,0:T(8,128)(2,1)} %get-tuple-element.129, s32[1024]{0:T(1024)S(1)} %pad_clamp_fusion.2), kind=kCustom, calls=%fused_computation.clone.1 | custom fusion | bytes 5243200 | tf_op jit(solution)/shard_map/while/body/eval_jaxpr/gather | solution.py:70
  200.4 0.1 iota_compare_fusion.2
  200.5 0.1 broadcast_bitcast_fusion.2
  200.6 0.9 fusion.37
  201.6 2.3 copy-done.1
  203.9 0.8 fusion.38
  204.7 2.7 %gather_fusion = bf16[80,128,128]{2,1,0:T(8,128)(2,1)S(1)} fusion(bf16[72,128,128]{2,1,0:T(8,128)(2,1)} %get-tuple-element.130, s32[1024]{0:T(1024)S(1)} %pad_clamp_fusion.2), kind=kCustom, calls=%fused_computation.1.clone.1 | custom fusion | bytes 5243200 | tf_op jit(solution)/shard_map/while/body/eval_jaxpr/gather | solution.py:71
  207.4 3.5 %fusion.39 = bf16[2,4,128,128]{3,2,1,0:T(8,128)(2,1)S(1)} fusion(bf16[2,4,128,128]{3,2,1,0:T(8,128)(2,1)S(1)} %get-tuple-element.117, s32[]{:T(128)} %get-tuple-element.116, bf16[4,2560,128]{2,1,0:T(8,128)(2,1)S(1)} %bitcast.67, f32[4,128,2560]{2,1,0:T(8,128)} %copy-done.1, f32[4,128]{1,0:T(4,128)S(1)} %get-tuple-element.107, f32[4,128]{1,0:T(4,128)S(1)} %fusion.38), kind=kOutput, calls=%fused_computation.11.clone.1 | convolution fusion | flops 338296832 | bytes 7999492 | tf_op jit(solution)/shard_map/while/body/eval_jaxpr/fve,fez->fvz/dot_general | solution.py:32
  211.0 31.4 %all_to_all.68 = bf16[8,128,128]{2,1,0:T(8,128)(2,1)S(1)} all-to-all(bf16[8,128,128]{2,1,0:T(8,128)(2,1)S(1)} %bitcast.80), channel_id=1, replica_groups=mesh['frame'=64,'head'=8] {'head'}, dimensions={0} | all-to-all | bytes 524288 | tf_op jit(solution)/shard_map/all_to_all | solution.py:83
  242.4 0.2 copy.20
  242.5 0.9 copy.21
  (32 shorter events, 0.7 us)
Async XLA Ops:
  0.0 69.1 %copy-start = (bf16[128,1024]{1,0:T(8,128)(2,1)S(1)}, bf16[128,1024]{1,0:T(8,128)(2,1)}, u32[]{:S(2)}) copy-start(bf16[128,1024]{1,0:T(8,128)(2,1)} %param.7) | copy-start | bytes 786436
  0.0 73.9 %copy-start.3 = (s32[1,8]{1,0:T(1,128)S(1)}, s32[1,8]{1,0:T(1,128)}, u32[]{:S(2)}) copy-start(s32[1,8]{1,0:T(1,128)} %param.11) | copy-start | bytes 100
  0.0 80.3 %copy-start.2 = (s32[1,8,20]{2,1,0:T(8,128)S(1)}, s32[1,8,20]{2,1,0:T(8,128)}, u32[]{:S(2)}) copy-start(s32[1,8,20]{2,1,0:T(8,128)} %param.10) | copy-start | bytes 1924
  2.0 41.2 %all-to-all-start.1 = ((bf16[128,8,128]{2,0,1:T(8,128)(2,1)}), bf16[128,8,128]{2,0,1:T(8,128)(2,1)S(1)}, u32[]{:S(2)}, u32[]{:S(2)}) async-start(bf16[128,8,128]{2,0,1:T(8,128)(2,1)} %copy.17), calls=%async_computation.1 | async-start | bytes 524288 | tf_op jit(solution)/shard_map/all_to_all | solution.py:44
  63.4 25.1 %collective-permute-start = (bf16[2,1024,128]{2,1,0:T(8,128)(2,1)S(1)}, bf16[2,1024,128]{2,1,0:T(8,128)(2,1)S(1)}, u32[]{:S(2)}, u32[]{:S(2)}) collective-permute-start(bf16[2,1024,128]{2,1,0:T(8,128)(2,1)S(1)} %pad_maximum_fusion), channel_id=1, source_target_pairs={{0,32},{8,40},{16,48},{24,56},{32,64},{40,72},{48,80},{56,88},{64,... | collective-permute-start | bytes 1572872 | tf_op jit(solution)/shard_map/ppermute | solution.py:17
  65.3 64.8 %collective-permute-start.1 = (bf16[2,1024,128]{2,1,0:T(8,128)(2,1)S(1)}, bf16[2,1024,128]{2,1,0:T(8,128)(2,1)S(1)}, u32[]{:S(2)}, u32[]{:S(2)}) collective-permute-start(bf16[2,1024,128]{2,1,0:T(8,128)(2,1)S(1)} %pad_maximum_fusion), channel_id=1, source_target_pairs={{0,24},{8,32},{16,40},{24,48},{32,56},{40,64},{48,72},{56,80},{64,... | collective-permute-start | bytes 1572872 | tf_op jit(solution)/shard_map/ppermute | solution.py:17
  67.2 64.9 %collective-permute-start.2 = (bf16[2,1024,128]{2,1,0:T(8,128)(2,1)S(1)}, bf16[2,1024,128]{2,1,0:T(8,128)(2,1)S(1)}, u32[]{:S(2)}, u32[]{:S(2)}) collective-permute-start(bf16[2,1024,128]{2,1,0:T(8,128)(2,1)S(1)} %pad_maximum_fusion), channel_id=1, source_target_pairs={{0,16},{8,24},{16,32},{24,40},{32,48},{40,56},{48,64},{56,72},{64,... | collective-permute-start | bytes 1572872 | tf_op jit(solution)/shard_map/ppermute | solution.py:17
  69.9 114.3 %all-to-all-start = ((bf16[128,8,128]{2,0,1:T(8,128)(2,1)}), bf16[128,8,128]{2,0,1:T(8,128)(2,1)S(1)}, u32[]{:S(2)}, u32[]{:S(2)}) async-start(bf16[128,8,128]{2,0,1:T(8,128)(2,1)} %copy_bitcast_fusion.1), calls=%async_computation | async-start | bytes 524288 | tf_op jit(solution)/shard_map/all_to_all | solution.py:43
  74.6 59.5 %collective-permute-start.3 = (bf16[2,1024,128]{2,1,0:T(8,128)(2,1)S(1)}, bf16[2,1024,128]{2,1,0:T(8,128)(2,1)S(1)}, u32[]{:S(2)}, u32[]{:S(2)}) collective-permute-start(bf16[2,1024,128]{2,1,0:T(8,128)(2,1)S(1)} %pad_maximum_fusion), channel_id=1, source_target_pairs={{0,8},{8,16},{16,24},{24,32},{32,40},{40,48},{48,56},{56,64},{64,7... | collective-permute-start | bytes 1572872 | tf_op jit(solution)/shard_map/ppermute | solution.py:17
  80.3 54.0 %collective-permute-start.4 = (bf16[2,1024,128]{2,1,0:T(8,128)(2,1)S(1)}, bf16[2,1024,128]{2,1,0:T(8,128)(2,1)S(1)}, u32[]{:S(2)}, u32[]{:S(2)}) collective-permute-start(bf16[2,1024,128]{2,1,0:T(8,128)(2,1)S(1)} %pad_maximum_fusion), channel_id=1, source_target_pairs={{8,0},{16,8},{24,16},{32,24},{40,32},{48,40},{56,48},{64,56},{72,6... | collective-permute-start | bytes 1572872 | tf_op jit(solution)/shard_map/ppermute | solution.py:17
  88.4 70.0 %collective-permute-start.5 = (bf16[2,1024,128]{2,1,0:T(8,128)(2,1)S(1)}, bf16[2,1024,128]{2,1,0:T(8,128)(2,1)S(1)}, u32[]{:S(2)}, u32[]{:S(2)}) collective-permute-start(bf16[2,1024,128]{2,1,0:T(8,128)(2,1)S(1)} %pad_maximum_fusion), channel_id=1, source_target_pairs={{16,0},{24,8},{32,16},{40,24},{48,32},{56,40},{64,48},{72,56},{80,... | collective-permute-start | bytes 1572872 | tf_op jit(solution)/shard_map/ppermute | solution.py:17
  130.1 45.0 %collective-permute-start.6 = (bf16[2,1024,128]{2,1,0:T(8,128)(2,1)S(1)}, bf16[2,1024,128]{2,1,0:T(8,128)(2,1)S(1)}, u32[]{:S(2)}, u32[]{:S(2)}) collective-permute-start(bf16[2,1024,128]{2,1,0:T(8,128)(2,1)S(1)} %pad_maximum_fusion), channel_id=1, source_target_pairs={{24,0},{32,8},{40,16},{48,24},{56,32},{64,40},{72,48},{80,56},{88,... | collective-permute-start | bytes 1572872 | tf_op jit(solution)/shard_map/ppermute | solution.py:17
  132.1 49.7 %collective-permute-start.7 = (bf16[2,1024,128]{2,1,0:T(8,128)(2,1)S(1)}, bf16[2,1024,128]{2,1,0:T(8,128)(2,1)S(1)}, u32[]{:S(2)}, u32[]{:S(2)}) collective-permute-start(bf16[2,1024,128]{2,1,0:T(8,128)(2,1)S(1)} %pad_maximum_fusion), channel_id=1, source_target_pairs={{32,0},{40,8},{48,16},{56,24},{64,32},{72,40},{80,48},{88,56},{96,... | collective-permute-start | bytes 1572872 | tf_op jit(solution)/shard_map/ppermute | solution.py:17
  188.2 2.3 copy-start.1
  201.6 2.3 copy-start.1
where the time goes:
time: 244 us; the launch traced here: 243 us
  starting transfers between devices  79 us (32%)
  waiting for transfers between devices  76.6 us (31%)
  blocking collectives  51.5 us (21%)
  local copies, waits for them, and re-layouts  24.4 us (10%)
  matrix products  8.95 us (4%)
  other arithmetic  2.63 us (1%)
    ppermute x8, starting transfers between devices, shifted(): return lax.ppermute(block, axis, route)  58.8 us
    ppermute x8, waiting for transfers between devices, shifted(): return lax.ppermute(block, axis, route)  53.5 us
    all_to_all x1, blocking collectives, body(): lax.all_to_all(outputs, 'head', split_axis=0, concat_axis=1, tiled=True)  31.4 us
    all_to_all x1, waiting for transfers between devices, body(): lax.all_to_all(key_vectors, 'head', split_axis=1, concat_axis=0, tiled=True)  23 us
    all_to_all x1, blocking collectives, body(): lax.all_to_all(value_vectors, 'head', split_axis=1, concat_axis=0, tiled=...  20.1 us
    all_to_all x1, starting transfers between devices, body(): lax.all_to_all(key_vectors, 'head', split_axis=1, concat_axis=0, tiled=True)  16.8 us
    dot_general x2, matrix products, masked_softmax(): jnp.einsum('fve,fez->fvz', exponent.astype(jnp.bfloat16), gathered_value_...  7.08 us
    gather x2, local copies, waits for them, and re-layouts, one_block(): value_tiles[block_ids].reshape(block_tiles, slot_count * TILE, HEAD_DIM)  5.44 us
  transfers between devices with their start and end apart: 10, of which 5 were waited for; matrix products, arithmetic and copies ran while one was open for 3% of the time, Pallas kernels for 0%

commit v1 on v0

v1 whole, which is shorter than its diff:
```python
import math

import jax
import jax.numpy as jnp
from jax import lax
from jax.experimental import pallas as pl
from jax.experimental.pallas import tpu as pltpu
from jax.sharding import PartitionSpec as P

TILE = 128
DIM = 128
SLOTS = 20
COLS = 32
PERX = 8
SUBS = 2
PIECE = 4 // SUBS
MESH = pl.DeviceIdType.MESH

DN1, DN2, UP1, UP2, SB0, SBD1, SBU1, SBD2, SBU2 = range(9)


def kernel(
    q_in, k_in, v_in, lists_in, live_in, out,
    kv, qs, os, scores, list_land, live_land, lists, live,
    a2a_send, a2a_recv, win_send, win_recv, out_send, out_recv, meta_send, meta_recv, meta_local,
):
    f, g = lax.axis_index("frame"), lax.axis_index("head")
    m, c = lax.div(f, 2), lax.rem(f, 2)
    x = lax.div(m, PERX)
    zh, y = lax.div(g, 4), lax.rem(g, 4)
    b = lax.rem(zh + x, 2)
    head = b * 4 + y

    def half_of(rel):
        return lax.rem(b + lax.div(lax.rem(m + rel + COLS, COLS), PERX), 2)

    def device(rel, core):
        return (lax.rem(m + rel + COLS, COLS) * 2 + core, half_of(rel) * 4 + y)

    up, down, sibling = device(1, c), device(-1, c), device(0, 1 - c)

    def owner(i):
        far = 1 - lax.div(i, 4)
        zh2 = lax.rem(zh + far, 2)
        y2 = lax.rem(y + lax.rem(i, 4) + (1 - far), 4)
        return zh2 * 4 + y2, lax.rem(zh2 + x, 2) * 4 + y2

    others = [owner(jnp.int32(i)) for i in range(7)]

    barrier = pltpu.get_barrier_semaphore()
    for target in [(f, o) for o, _ in others] + [up, down, sibling]:
        pl.semaphore_signal(barrier, inc=1, device_id=target, device_id_type=MESH)
    pl.semaphore_wait(barrier, 10)

    started = []

    def remote(src, dst, send, recv, target):
        copy = pltpu.make_async_remote_copy(
            src_ref=src, dst_ref=dst, send_sem=send, recv_sem=recv, device_id=target, device_id_type=MESH
        )
        copy.start()
        return copy

    def columns(h):
        return pl.ds(pl.multiple_of(h * DIM, DIM), DIM)

    slot0 = 32 + c * 8
    ins = (k_in, v_in, q_in)

    def landing(t, j):
        return qs.at[j] if t == 2 else kv.at[slot0 + j, t]

    def exchange(i, t):
        o, h = others[i]
        started.append(
            remote(ins[t].at[:, columns(h)], landing(t, g), a2a_send.at[i, t], a2a_recv.at[g, t], (f, o))
        )

    def arrived(t, j):
        dst = landing(t, j)
        pltpu.make_async_copy(dst, dst, a2a_recv.at[j, t]).wait()

    for i in range(4):
        exchange(i, 0)
        exchange(i, 1)
    for i in range(4, 7):
        exchange(i, 0)
        exchange(i, 1)
    for t in range(3):
        pltpu.make_async_copy(ins[t].at[:, columns(head)], landing(t, g), a2a_recv.at[g, t]).start()
    for i in range(4, 7):
        exchange(i, 2)

    across = (f, lax.rem(g + 4, 8))
    started.append(remote(lists_in, list_land, meta_send.at[0], meta_recv.at[0], across))
    started.append(remote(live_in, live_land, meta_send.at[1], meta_recv.at[1], across))
    own_lists = pltpu.make_async_copy(lists_in.at[0], lists.at[0], meta_local.at[0])
    own_live = pltpu.make_async_copy(live_in, live.at[pl.ds(0, 1)], meta_local.at[1])
    own_lists.start()
    own_live.start()

    def tiles(rel, core, o, s):
        first = lax.rem(half_of(rel) + o, 2) * 4 + s * PIECE
        return pl.ds((rel + 2) * 16 + core * 8 + first, PIECE)

    def window_copy(kind, rel_src, rel_dst, o, s, target):
        src = tiles(rel_src, c, o, s)
        first = src.start - (rel_src + 2) * 16 + (rel_dst + 2) * 16
        return pltpu.make_async_remote_copy(
            src_ref=kv.at[src],
            dst_ref=kv.at[pl.ds(first, PIECE)],
            send_sem=win_send.at[kind, o, s],
            recv_sem=win_recv.at[kind, o, s],
            device_id=target,
            device_id_type=MESH,
        )

    def pass_on(kind, rel_src, rel_dst, o, s, target):
        copy = window_copy(kind, rel_src, rel_dst, o, s, target)
        copy.start()
        started.append(copy)

    def window_wait(kind, rel, core, o, s):
        dst = kv.at[tiles(rel, core, o, s)]
        pltpu.make_async_copy(dst, dst, win_recv.at[kind, o, s]).wait()

    for o in range(2):
        for s in range(SUBS):
            for p in range(PIECE):
                j = lax.rem(zh + o, 2) * 4 + s * PIECE + p
                arrived(0, j)
                arrived(1, j)
            pass_on(DN1, 0, -1, o, s, up)
            pass_on(UP1, 0, 1, o, s, down)
            pass_on(SB0, 0, 0, o, s, sibling)
        if o == 1:
            for i in range(4):
                exchange(i, 2)
        for s in range(SUBS):
            window_wait(DN1, -1, c, o, s)
            pass_on(DN2, -1, -2, o, s, up)
            pass_on(SBD1, -1, -1, o, s, sibling)
            window_wait(UP1, 1, c, o, s)
            pass_on(UP2, 1, 2, o, s, down)
            pass_on(SBU1, 1, 1, o, s, sibling)

    for o in range(2):
        for s in range(SUBS):
            window_wait(DN2, -2, c, o, s)

            @pl.when(c == 1)
            def _():
                window_copy(SBD2, -2, -2, o, s, sibling).start()

            window_wait(UP2, 2, c, o, s)

            @pl.when(c == 0)
            def _():
                window_copy(SBU2, 2, 2, o, s, sibling).start()

    for o in range(2):
        for s in range(SUBS):
            for kind, rel in ((SB0, 0), (SBD1, -1), (SBU1, 1)):
                window_wait(kind, rel, 1 - c, o, s)

            @pl.when(c == 0)
            def _():
                window_wait(SBD2, -2, 1, o, s)
                window_copy(SBU2, 2, 2, o, s, sibling).wait_send()

            @pl.when(c == 1)
            def _():
                window_wait(SBU2, 2, 0, o, s)
                window_copy(SBD2, -2, -2, o, s, sibling).wait_send()

    pltpu.make_async_copy(list_land, list_land, meta_recv.at[0]).wait()
    pltpu.make_async_copy(live_land, live_land, meta_recv.at[1]).wait()
    own_lists.wait()
    own_live.wait()
    crossed_lists = pltpu.make_async_copy(list_land.at[0], lists.at[1], meta_local.at[2])
    crossed_live = pltpu.make_async_copy(live_land, live.at[pl.ds(1, 1)], meta_local.at[3])
    crossed_lists.start()
    crossed_live.start()
    crossed_lists.wait()
    crossed_live.wait()

    odd = lax.rem(x, 2)
    base = (m - 2) * 16
    factor = math.log2(math.e) / math.sqrt(DIM)

    def attend(i, carry):
        j, _ = owner(i)
        arrived(2, j)
        query = qs[j]
        ids = [jnp.clip(lists[odd, j, s] - base, 0, 79) for s in range(SLOTS)]
        count = live[odd, j]
        peak = jnp.full((TILE, 2 * TILE), -jnp.inf, jnp.float32)
        for s in range(0, SLOTS, 2):
            pair = jnp.concatenate([kv[ids[s], 0], kv[ids[s + 1], 0]], axis=0)
            raw = lax.dot_general(query, pair, (((1,), (1,)), ((), ())), preferred_element_type=jnp.float32)
            scores[s // 2] = raw
            peak = jnp.maximum(peak, raw)
        top = jnp.max(peak, axis=1, keepdims=True) * factor
        total = jnp.zeros((TILE, 2 * TILE), jnp.float32)
        acc = jnp.zeros((TILE, DIM), jnp.float32)
        lane = lax.broadcasted_iota(jnp.int32, (1, 2 * TILE), 1)
        for s in range(0, SLOTS, 2):
            dead = jnp.where(s + lax.div(lane, TILE) < count, 0.0, jnp.inf)
            weight = jnp.exp2(scores[s // 2] * factor - (top + dead))
            total = total + weight
            pair = jnp.concatenate([kv[ids[s], 1], kv[ids[s + 1], 1]], axis=0)
            acc = acc + jnp.dot(weight.astype(jnp.bfloat16), pair, preferred_element_type=jnp.float32)
        os[j] = (acc / jnp.sum(total, axis=1, keepdims=True)).astype(jnp.bfloat16)

        @pl.when(i < 7)
        def _():
            remote(os.at[j], out.at[:, columns(head)], out_send.at[j], out_recv.at[g], (f, j))

        @pl.when(i == 7)
        def _():
            pltpu.make_async_copy(os.at[j], out.at[:, columns(head)], out_recv.at[g]).start()

        return carry

    lax.fori_loop(0, 8, attend, 0)

    for copy in started:
        copy.wait_send()
    for o, _ in others:
        pltpu.make_async_copy(os.at[o], os.at[o], out_send.at[o]).wait()
    for o, h in others + [(g, head)]:
        dst = out.at[:, columns(h)]
        pltpu.make_async_copy(dst, dst, out_recv.at[o]).wait()


def body(queries, key_vectors, value_vectors, tile_lists, live_slots):
    dma = pltpu.SemaphoreType.DMA
    hbm = pl.BlockSpec(memory_space=pl.ANY)
    bf16, i32 = jnp.bfloat16, jnp.int32
    return pl.pallas_call(
        kernel,
        out_shape=jax.ShapeDtypeStruct(queries.shape, queries.dtype),
        in_specs=[hbm] * 5,
        out_specs=hbm,
        scratch_shapes=[
            pltpu.VMEM((80, 2, TILE, DIM), bf16),
            pltpu.VMEM((8, TILE, DIM), bf16),
            pltpu.VMEM((8, TILE, DIM), bf16),
            pltpu.VMEM((SLOTS // 2, TILE, 2 * TILE), jnp.float32),
            pltpu.VMEM(tile_lists.shape, i32),
            pltpu.VMEM(live_slots.shape, i32),
            pltpu.SMEM((2,) + tile_lists.shape[1:], i32),
            pltpu.SMEM((2, live_slots.shape[1]), i32),
            dma((7, 3)),
            dma((8, 3)),
            dma((9, 2, SUBS)),
            dma((9, 2, SUBS)),
            dma((8,)),
            dma((8,)),
            dma((2,)),
            dma((2,)),
            dma((4,)),
        ],
        compiler_params=pltpu.CompilerParams(
            collective_id=0, has_side_effects=True, vmem_limit_bytes=32 << 20
        ),
    )(queries, key_vectors, value_vectors, tile_lists, live_slots)


def solution(mesh):
    placed = (
        P(("frame", "head"), None),
        P(("frame", "head"), None),
        P(("frame", "head"), None),
        P("head", "frame", None),
        P("head", "frame"),
    )
    return jax.shard_map(
        body, mesh=mesh, in_specs=placed, out_specs=P(("frame", "head"), None), check_vma=False
    )
```

time: 244 us -> 105 us (0.43)
  the two profiles are of different devices: /device:TPU:36 before, /device:TPU:1 now
where the time goes in v1:
time: 105 us
  Pallas kernels  99.7 us (95%)
  local copies, waits for them, and re-layouts  4.89 us (5%)
    pallas_call x1, Pallas kernels, body(): pl.pallas_call(kernel, out_shape=jax.ShapeDtypeStruct(queries.shape, quer...  99.7 us
    unnamed x11, local copies, waits for them, and re-layouts  4.89 us

profile of v1, /device:TPU:1, one launch (start us, length us, event | category | flops | bytes accessed | tf_op | source)
XLA Modules:
  0.0 104.6 jit_solution(17577703268006755609)
XLA Ops:
  0.0 0.0 copy-start
  0.0 0.9 copy-done
  1.0 0.0 copy-start.1
  1.0 0.9 copy-done.1
  1.9 0.0 copy-start.2
  1.9 0.9 copy-done.2
  2.9 0.0 copy-start.3
  2.9 0.7 copy-done.3
  3.5 0.0 copy-start.4
  3.5 0.7 copy-done.4
  4.2 99.7 %shard_map.55 = bf16[128,1024]{1,0:T(8,128)(2,1)S(1)} custom-call(bf16[128,1024]{1,0:T(8,128)(2,1)S(1)} %copy-done, bf16[128,1024]{1,0:T(8,128)(2,1)S(1)} %copy-done.1, bf16[128,1024]{1,0:T(8,128)(2,1)S(1)} %copy-done.2, s32[1,8,20]{2,1,0:T(8,128)S(1)} %copy-done.3, s32[1,8]{1,0:T(1,128)S(1)} %copy-done.4), custom_call_target="tpu_custom_call" | custom-call | tf_op jit(solution)/shard_map/pallas_call | solution.py:240
  103.9 0.7 copy.7
Async XLA Ops:
  0.0 0.9 copy-start
  1.0 0.9 copy-start.1
  1.9 0.9 copy-start.2
  2.9 0.7 copy-start.3
  3.5 0.7 copy-start.4

commit v2 on v1

--- a/solution.py
+++ b/solution.py
@@ -133,9 +133,6 @@
             pass_on(DN1, 0, -1, o, s, up)
             pass_on(UP1, 0, 1, o, s, down)
             pass_on(SB0, 0, 0, o, s, sibling)
-        if o == 1:
-            for i in range(4):
-                exchange(i, 2)
         for s in range(SUBS):
             window_wait(DN1, -1, c, o, s)
             pass_on(DN2, -1, -2, o, s, up)
@@ -143,6 +140,9 @@
             window_wait(UP1, 1, c, o, s)
             pass_on(UP2, 1, 2, o, s, down)
             pass_on(SBU1, 1, 1, o, s, sibling)
+
+    for i in range(4):
+        exchange(i, 2)
 
     for o in range(2):
         for s in range(SUBS):
@@ -235,7 +235,7 @@
 
 def body(queries, key_vectors, value_vectors, tile_lists, live_slots):
     dma = pltpu.SemaphoreType.DMA
-    hbm = pl.BlockSpec(memory_space=pl.ANY)
+    hbm = pl.BlockSpec(memory_space=pltpu.HBM)
     bf16, i32 = jnp.bfloat16, jnp.int32
     return pl.pallas_call(
         kernel,
@@ -262,7 +262,7 @@
             dma((4,)),
         ],
         compiler_params=pltpu.CompilerParams(
-            collective_id=0, has_side_effects=True, vmem_limit_bytes=32 << 20
+            collective_id=0, has_side_effects=True, vmem_limit_bytes=63 << 20
         ),
     )(queries, key_vectors, value_vectors, tile_lists, live_slots)
 

time: 105 us -> 97.8 us (0.931)
  Pallas kernels: 99.7 us -> 95.9 us
  local copies, waits for them, and re-layouts: 4.89 us -> 1.67 us
    pallas_call x1, Pallas kernels: 99.7 us -> 95.9 us  [body(): pl.pallas_call(kernel, out_shape=jax.ShapeDtypeStruct(queries.shape, quer...]
    unnamed x11 -> x1, local copies, waits for them, and re-layouts: 4.89 us -> 1.67 us
where the time goes in v2:
time: 97.8 us; the launch traced here: 97.6 us
  Pallas kernels  95.9 us (98%)
  local copies, waits for them, and re-layouts  1.67 us (2%)
    pallas_call x1, Pallas kernels, body(): pl.pallas_call(kernel, out_shape=jax.ShapeDtypeStruct(queries.shape, quer...  95.9 us

profile of v2, /device:TPU:1, one launch (start us, length us, event | category | flops | bytes accessed | tf_op | source)
XLA Modules:
  0.0 97.6 jit_solution(15742692892012410653)
XLA Ops:
  0.0 95.9 %shard_map.55 = bf16[128,1024]{1,0:T(8,128)(2,1)} custom-call(bf16[128,1024]{1,0:T(8,128)(2,1)} %q_in.1, bf16[128,1024]{1,0:T(8,128)(2,1)} %k_in.1, bf16[128,1024]{1,0:T(8,128)(2,1)} %v_in.1, s32[1,8,20]{2,1,0:T(8,128)} %lists_in.1, s32[1,8]{1,0:T(1,128)} %live_in.1), custom_call_target="tpu_custom_call" | custom-call | tf_op jit(solution)/shard_map/pallas_call | solution.py:240
  95.9 1.7 %copy.7 = bf16[128,1024]{1,0:T(8,128)(2,1)} copy(bf16[128,1024]{1,0:T(8,128)(2,1)} %shard_map.55) | data formatting | bytes 524288

commit v3 on v2

--- a/solution.py
+++ b/solution.py
@@ -23,6 +23,7 @@
     q_in, k_in, v_in, lists_in, live_in, out,
     kv, qs, os, scores, list_land, live_land, lists, live,
     a2a_send, a2a_recv, win_send, win_recv, out_send, out_recv, meta_send, meta_recv, meta_local,
+    far_send, far_recv, chain_send, chain_recv, sib_send, sib_recv,
 ):
     f, g = lax.axis_index("frame"), lax.axis_index("head")
     m, c = lax.div(f, 2), lax.rem(f, 2)
@@ -45,12 +46,27 @@
         y2 = lax.rem(y + lax.rem(i, 4) + (1 - far), 4)
         return zh2 * 4 + y2, lax.rem(zh2 + x, 2) * 4 + y2
 
-    others = [owner(jnp.int32(i)) for i in range(7)]
-
+    def fixed_owner(i):
+        far = 1 - i // 4
+        zh2 = lax.rem(zh + far, 2)
+        y2 = lax.rem(y + i % 4 + (1 - far), 4)
+        return zh2 * 4 + y2, lax.rem(zh2 + x, 2) * 4 + y2
+
+    others = [fixed_owner(i) for i in range(7)]
+
+    def across_to(rel, y2):
+        column = lax.rem(m + rel + COLS, COLS)
+        return (column * 2 + c, lax.rem(1 - b + lax.div(column, PERX), 2) * 4 + y2)
+
+    rows = [lax.rem(y + i, 4) for i in range(4)]
     barrier = pltpu.get_barrier_semaphore()
-    for target in [(f, o) for o, _ in others] + [up, down, sibling]:
+    for target in (
+        [(f, o) for o, _ in others]
+        + [up, down, sibling]
+        + [across_to(rel, y2) for rel in (-2, 2) for y2 in rows]
+    ):
         pl.semaphore_signal(barrier, inc=1, device_id=target, device_id_type=MESH)
-    pl.semaphore_wait(barrier, 10)
+    pl.semaphore_wait(barrier, 18)
 
     started = []
 
@@ -80,9 +96,11 @@
         dst = landing(t, j)
         pltpu.make_async_copy(dst, dst, a2a_recv.at[j, t]).wait()
 
-    for i in range(4):
-        exchange(i, 0)
-        exchange(i, 1)
+    for i, y2 in enumerate(rows):
+        for t, rel in ((0, 2), (1, -2)):
+            src = ins[t].at[:, columns((1 - b) * 4 + y2)]
+            dst = kv.at[(rel + 2) * 16 + c * 8 + g, t]
+            started.append(remote(src, dst, far_send.at[i, t], far_recv.at[y, t], across_to(-rel, y2)))
     for i in range(4, 7):
         exchange(i, 0)
         exchange(i, 1)
@@ -99,9 +117,11 @@
     own_lists.start()
     own_live.start()
 
+    def first_tile(rel, o, s):
+        return lax.rem(half_of(rel) + o, 2) * 4 + s * PIECE
+
     def tiles(rel, core, o, s):
-        first = lax.rem(half_of(rel) + o, 2) * 4 + s * PIECE
-        return pl.ds((rel + 2) * 16 + core * 8 + first, PIECE)
+        return pl.ds((rel + 2) * 16 + core * 8 + first_tile(rel, o, s), PIECE)
 
     def window_copy(kind, rel_src, rel_dst, o, s, target):
         src = tiles(rel_src, c, o, s)
@@ -124,27 +144,99 @@
         dst = kv.at[tiles(rel, core, o, s)]
         pltpu.make_async_copy(dst, dst, win_recv.at[kind, o, s]).wait()
 
-    for o in range(2):
+    def own(o, s):
+        for p in range(PIECE):
+            j = first_tile(0, o, s) + p
+            arrived(0, j)
+            arrived(1, j)
+        pass_on(DN1, 0, -1, o, s, up)
+        pass_on(UP1, 0, 1, o, s, down)
+        pass_on(SB0, 0, 0, o, s, sibling)
+
+    def then(o, s):
+        window_wait(DN1, -1, c, o, s)
+        pass_on(DN2, -1, -2, o, s, up)
+        pass_on(SBD1, -1, -1, o, s, sibling)
+        window_wait(UP1, 1, c, o, s)
+        pass_on(UP2, 1, 2, o, s, down)
+        pass_on(SBU1, 1, 1, o, s, sibling)
+
+    def chain_tiles(rel, core, t, s, to):
+        return kv.at[pl.ds((to + 2) * 16 + core * 8 + first_tile(rel, 1, s), PIECE), t]
+
+    def chain(stage):
         for s in range(SUBS):
-            for p in range(PIECE):
-                j = lax.rem(zh + o, 2) * 4 + s * PIECE + p
-                arrived(0, j)
-                arrived(1, j)
-            pass_on(DN1, 0, -1, o, s, up)
-            pass_on(UP1, 0, 1, o, s, down)
-            pass_on(SB0, 0, 0, o, s, sibling)
-        for s in range(SUBS):
-            window_wait(DN1, -1, c, o, s)
-            pass_on(DN2, -1, -2, o, s, up)
-            pass_on(SBD1, -1, -1, o, s, sibling)
-            window_wait(UP1, 1, c, o, s)
-            pass_on(UP2, 1, 2, o, s, down)
-            pass_on(SBU1, 1, 1, o, s, sibling)
-
-    for i in range(4):
-        exchange(i, 2)
-
-    for o in range(2):
+            for t, rel, step, target in ((0, 2 - stage, -1, up), (1, stage - 2, 1, down)):
+                if stage == 0:
+                    for e in range(PIECE):
+                        dst = kv.at[(rel + 2) * 16 + c * 8 + first_tile(rel, 1, s) + e, t]
+                        pltpu.make_async_copy(dst, dst, far_recv.at[s * PIECE + e, t]).wait()
+                else:
+                    dst = chain_tiles(rel, c, t, s, rel)
+                    pltpu.make_async_copy(dst, dst, chain_recv.at[stage - 1, t, s]).wait()
+                if stage < 4:
+                    src, dst = chain_tiles(rel, c, t, s, rel), chain_tiles(rel, c, t, s, rel + step)
+                    started.append(remote(src, dst, chain_send.at[stage, t, s], chain_recv.at[stage, t, s], target))
+                if abs(rel) < 2:
+                    share(stage, t, rel, s).start()
+                else:
+                    pl.when(c == (0 if rel == 2 else 1))(share(stage, t, rel, s).start)
+
+    def share(stage, t, rel, s):
+        src = chain_tiles(rel, c, t, s, rel)
+        return pltpu.make_async_remote_copy(
+            src_ref=src,
+            dst_ref=src,
+            send_sem=sib_send.at[stage, t, s],
+            recv_sem=sib_recv.at[stage, t, s],
+            device_id=sibling,
+            device_id_type=MESH,
+        )
+
+    def shared(stage, t, rel, s):
+        dst = chain_tiles(rel, 1 - c, t, s, rel)
+        wait = pltpu.make_async_copy(dst, dst, sib_recv.at[stage, t, s]).wait
+        if abs(rel) < 2:
+            wait()
+            share(stage, t, rel, s).wait_send()
+        else:
+            sender = c == (0 if rel == 2 else 1)
+            pl.when(sender)(share(stage, t, rel, s).wait_send)
+            pl.when(jnp.logical_not(sender))(wait)
+
+    q_copies = [
+        pltpu.make_async_remote_copy(
+            src_ref=q_in.at[:, columns(h)],
+            dst_ref=qs.at[g],
+            send_sem=a2a_send.at[i, 2],
+            recv_sem=a2a_recv.at[g, 2],
+            device_id=(f, o),
+            device_id_type=MESH,
+        )
+        for i, (o, h) in enumerate(others[:4])
+    ]
+    started.extend(q_copies)
+
+    def q_far(*some):
+        for i in some:
+            q_copies[i].start()
+
+    soon = lax.rem(m, PERX) < 3
+    for s in range(SUBS):
+        own(0, s)
+    for s in range(SUBS):
+        then(0, s)
+    chain(0)
+    chain(1)
+    chain(2)
+
+    chain(3)
+
+    pl.when(soon)(lambda: q_far(0, 1, 2, 3))
+    chain(4)
+
+    pl.when(jnp.logical_not(soon))(lambda: q_far(0, 1, 2, 3))
+    for o in (0,):
         for s in range(SUBS):
             window_wait(DN2, -2, c, o, s)
 
@@ -158,7 +250,7 @@
             def _():
                 window_copy(SBU2, 2, 2, o, s, sibling).start()
 
-    for o in range(2):
+    for o in (0,):
         for s in range(SUBS):
             for kind, rel in ((SB0, 0), (SBD1, -1), (SBU1, 1)):
                 window_wait(kind, rel, 1 - c, o, s)
@@ -172,6 +264,11 @@
             def _():
                 window_wait(SBU2, 2, 0, o, s)
                 window_copy(SBD2, -2, -2, o, s, sibling).wait_send()
+
+    for stage in range(5):
+        for s in range(SUBS):
+            shared(stage, 0, 2 - stage, s)
+            shared(stage, 1, stage - 2, s)
 
     pltpu.make_async_copy(list_land, list_land, meta_recv.at[0]).wait()
     pltpu.make_async_copy(live_land, live_land, meta_recv.at[1]).wait()
@@ -188,7 +285,10 @@
     base = (m - 2) * 16
     factor = math.log2(math.e) / math.sqrt(DIM)
 
+    turn = jnp.where(lax.rem(m, PERX) >= 3, 4, 0)
+
     def attend(i, carry):
+        i = lax.rem(i + turn, 8)
         j, _ = owner(i)
         arrived(2, j)
         query = qs[j]
@@ -260,6 +360,12 @@
             dma((2,)),
             dma((2,)),
             dma((4,)),
+            dma((4, 2)),
+            dma((4, 2)),
+            dma((4, 2, SUBS)),
+            dma((4, 2, SUBS)),
+            dma((5, 2, SUBS)),
+            dma((5, 2, SUBS)),
         ],
         compiler_params=pltpu.CompilerParams(
             collective_id=0, has_side_effects=True, vmem_limit_bytes=63 << 20

time: 97.8 us -> 96.1 us (0.983)
  Pallas kernels: 95.9 us -> 94.3 us
    pallas_call x1, Pallas kernels: 95.9 us -> 94.3 us  [body(): pl.pallas_call(kernel, out_shape=jax.ShapeDtypeStruct(queries.shape, quer...]
where the time goes in v3:
time: 96.1 us; the launch traced here: 95.9 us
  Pallas kernels  94.3 us (98%)
  local copies, waits for them, and re-layouts  1.67 us (2%)
    pallas_call x1, Pallas kernels, body(): pl.pallas_call(kernel, out_shape=jax.ShapeDtypeStruct(queries.shape, quer...  94.3 us

profile of v3, /device:TPU:1, one launch (start us, length us, event | category | flops | bytes accessed | tf_op | source)
XLA Modules:
  0.0 95.9 jit_solution(2860316709421308961)
XLA Ops:
  0.0 94.3 %shard_map.55 = bf16[128,1024]{1,0:T(8,128)(2,1)} custom-call(bf16[128,1024]{1,0:T(8,128)(2,1)} %q_in.1, bf16[128,1024]{1,0:T(8,128)(2,1)} %k_in.1, bf16[128,1024]{1,0:T(8,128)(2,1)} %v_in.1, s32[1,8,20]{2,1,0:T(8,128)} %lists_in.1, s32[1,8]{1,0:T(1,128)} %live_in.1), custom_call_target="tpu_custom_call" | custom-call | tf_op jit(solution)/shard_map/pallas_call | solution.py:340
  94.3 1.7 %copy.7 = bf16[128,1024]{1,0:T(8,128)(2,1)} copy(bf16[128,1024]{1,0:T(8,128)(2,1)} %shard_map.55) | data formatting | bytes 524288

commit v4 on v3

--- a/solution.py
+++ b/solution.py
@@ -61,12 +61,12 @@
     rows = [lax.rem(y + i, 4) for i in range(4)]
     barrier = pltpu.get_barrier_semaphore()
     for target in (
-        [(f, o) for o, _ in others]
+        [(f, o) for o, _ in others[4:]]
         + [up, down, sibling]
         + [across_to(rel, y2) for rel in (-2, 2) for y2 in rows]
     ):
         pl.semaphore_signal(barrier, inc=1, device_id=target, device_id_type=MESH)
-    pl.semaphore_wait(barrier, 18)
+    pl.semaphore_wait(barrier, 14)
 
     started = []
 
@@ -110,8 +110,6 @@
         exchange(i, 2)
 
     across = (f, lax.rem(g + 4, 8))
-    started.append(remote(lists_in, list_land, meta_send.at[0], meta_recv.at[0], across))
-    started.append(remote(live_in, live_land, meta_send.at[1], meta_recv.at[1], across))
     own_lists = pltpu.make_async_copy(lists_in.at[0], lists.at[0], meta_local.at[0])
     own_live = pltpu.make_async_copy(live_in, live.at[pl.ds(0, 1)], meta_local.at[1])
     own_lists.start()
@@ -224,18 +222,19 @@
     soon = lax.rem(m, PERX) < 3
     for s in range(SUBS):
         own(0, s)
+    chain(0)
     for s in range(SUBS):
         then(0, s)
-    chain(0)
     chain(1)
+    q_far(0)
     chain(2)
-
+    q_far(1)
+    started.append(remote(lists_in, list_land, meta_send.at[0], meta_recv.at[0], across))
+    started.append(remote(live_in, live_land, meta_send.at[1], meta_recv.at[1], across))
     chain(3)
-
-    pl.when(soon)(lambda: q_far(0, 1, 2, 3))
+    q_far(2, 3)
     chain(4)
 
-    pl.when(jnp.logical_not(soon))(lambda: q_far(0, 1, 2, 3))
     for o in (0,):
         for s in range(SUBS):
             window_wait(DN2, -2, c, o, s)

time: 96.1 us -> 94 us (0.978)
  Pallas kernels: 94.3 us -> 92.1 us
    pallas_call x1, Pallas kernels: 94.3 us -> 92.1 us  [body(): pl.pallas_call(kernel, out_shape=jax.ShapeDtypeStruct(queries.shape, quer...]
where the time goes in v4:
time: 94 us; the launch traced here: 93.8 us
  Pallas kernels  92.1 us (98%)
  local copies, waits for them, and re-layouts  1.67 us (2%)
    pallas_call x1, Pallas kernels, body(): pl.pallas_call(kernel, out_shape=jax.ShapeDtypeStruct(queries.shape, quer...  92.1 us

profile of v4, /device:TPU:1, one launch (start us, length us, event | category | flops | bytes accessed | tf_op | source)
XLA Modules:
  0.0 93.8 jit_solution(1964987465184046108)
XLA Ops:
  0.0 92.1 %shard_map.55 = bf16[128,1024]{1,0:T(8,128)(2,1)} custom-call(bf16[128,1024]{1,0:T(8,128)(2,1)} %q_in.1, bf16[128,1024]{1,0:T(8,128)(2,1)} %k_in.1, bf16[128,1024]{1,0:T(8,128)(2,1)} %v_in.1, s32[1,8,20]{2,1,0:T(8,128)} %lists_in.1, s32[1,8]{1,0:T(1,128)} %live_in.1), custom_call_target="tpu_custom_call" | custom-call | tf_op jit(solution)/shard_map/pallas_call | solution.py:339
  92.1 1.7 %copy.7 = bf16[128,1024]{1,0:T(8,128)(2,1)} copy(bf16[128,1024]{1,0:T(8,128)(2,1)} %shard_map.55) | data formatting | bytes 524288

commit v5 on v4

--- a/solution.py
+++ b/solution.py
@@ -219,7 +219,6 @@
         for i in some:
             q_copies[i].start()
 
-    soon = lax.rem(m, PERX) < 3
     for s in range(SUBS):
         own(0, s)
     chain(0)
@@ -284,10 +283,7 @@
     base = (m - 2) * 16
     factor = math.log2(math.e) / math.sqrt(DIM)
 
-    turn = jnp.where(lax.rem(m, PERX) >= 3, 4, 0)
-
     def attend(i, carry):
-        i = lax.rem(i + turn, 8)
         j, _ = owner(i)
         arrived(2, j)
         query = qs[j]

time: 94 us -> 92.7 us (0.986); the launches traced: 93.8 us -> 91.1 us
  Pallas kernels: 92.1 us -> 89.4 us
    pallas_call x1, Pallas kernels: 92.1 us -> 89.4 us  [body(): pl.pallas_call(kernel, out_shape=jax.ShapeDtypeStruct(queries.shape, quer...]
where the time goes in v5:
time: 92.7 us; the launch traced here: 91.1 us
  Pallas kernels  89.4 us (96%)
  local copies, waits for them, and re-layouts  1.67 us (2%)
    pallas_call x1, Pallas kernels, body(): pl.pallas_call(kernel, out_shape=jax.ShapeDtypeStruct(queries.shape, quer...  89.4 us

profile of v5, /device:TPU:1, one launch (start us, length us, event | category | flops | bytes accessed | tf_op | source)
XLA Modules:
  0.0 91.1 jit_solution(9401289030806308072)
XLA Ops:
  0.0 89.4 %shard_map.55 = bf16[128,1024]{1,0:T(8,128)(2,1)} custom-call(bf16[128,1024]{1,0:T(8,128)(2,1)} %q_in.1, bf16[128,1024]{1,0:T(8,128)(2,1)} %k_in.1, bf16[128,1024]{1,0:T(8,128)(2,1)} %v_in.1, s32[1,8,20]{2,1,0:T(8,128)} %lists_in.1, s32[1,8]{1,0:T(1,128)} %live_in.1), custom_call_target="tpu_custom_call" | custom-call | tf_op jit(solution)/shard_map/pallas_call | solution.py:335
  89.5 1.7 %copy.7 = bf16[128,1024]{1,0:T(8,128)(2,1)} copy(bf16[128,1024]{1,0:T(8,128)(2,1)} %shard_map.55) | data formatting | bytes 524288

commit v6 on v5

--- a/solution.py
+++ b/solution.py
@@ -225,13 +225,13 @@
     for s in range(SUBS):
         then(0, s)
     chain(1)
-    q_far(0)
+    q_far(0, 1)
     chain(2)
-    q_far(1)
+    q_far(2)
     started.append(remote(lists_in, list_land, meta_send.at[0], meta_recv.at[0], across))
     started.append(remote(live_in, live_land, meta_send.at[1], meta_recv.at[1], across))
     chain(3)
-    q_far(2, 3)
+    q_far(3)
     chain(4)
 
     for o in (0,):

time: 92.7 us -> 92.7 us (level); the launches traced: 91.1 us -> 92.5 us
  Pallas kernels: 89.4 us -> 90.9 us
    pallas_call x1, Pallas kernels: 89.4 us -> 90.9 us  [body(): pl.pallas_call(kernel, out_shape=jax.ShapeDtypeStruct(queries.shape, quer...]
where the time goes in v6:
time: 92.7 us; the launch traced here: 92.5 us
  Pallas kernels  90.9 us (98%)
  local copies, waits for them, and re-layouts  1.67 us (2%)
    pallas_call x1, Pallas kernels, body(): pl.pallas_call(kernel, out_shape=jax.ShapeDtypeStruct(queries.shape, quer...  90.9 us

profile of v6, /device:TPU:1, one launch (start us, length us, event | category | flops | bytes accessed | tf_op | source)
XLA Modules:
  0.0 92.5 jit_solution(11930287504512557059)
XLA Ops:
  0.0 90.9 %shard_map.55 = bf16[128,1024]{1,0:T(8,128)(2,1)} custom-call(bf16[128,1024]{1,0:T(8,128)(2,1)} %q_in.1, bf16[128,1024]{1,0:T(8,128)(2,1)} %k_in.1, bf16[128,1024]{1,0:T(8,128)(2,1)} %v_in.1, s32[1,8,20]{2,1,0:T(8,128)} %lists_in.1, s32[1,8]{1,0:T(1,128)} %live_in.1), custom_call_target="tpu_custom_call" | custom-call | tf_op jit(solution)/shard_map/pallas_call | solution.py:335
  90.9 1.7 %copy.7 = bf16[128,1024]{1,0:T(8,128)(2,1)} copy(bf16[128,1024]{1,0:T(8,128)(2,1)} %shard_map.55) | data formatting | bytes 524288

commit v7 on v5

--- a/solution.py
+++ b/solution.py
@@ -106,8 +106,6 @@
         exchange(i, 1)
     for t in range(3):
         pltpu.make_async_copy(ins[t].at[:, columns(head)], landing(t, g), a2a_recv.at[g, t]).start()
-    for i in range(4, 7):
-        exchange(i, 2)
 
     across = (f, lax.rem(g + 4, 8))
     own_lists = pltpu.make_async_copy(lists_in.at[0], lists.at[0], meta_local.at[0])
@@ -221,6 +219,8 @@
 
     for s in range(SUBS):
         own(0, s)
+    for i in range(4, 7):
+        exchange(i, 2)
     chain(0)
     for s in range(SUBS):
         then(0, s)

time: 92.7 us -> 92.7 us (level)
  no operation moved by 1% of the time
where the time goes in v7:
time: 92.7 us; the launch traced here: 91.1 us
  Pallas kernels  89.5 us (97%)
  local copies, waits for them, and re-layouts  1.67 us (2%)
    pallas_call x1, Pallas kernels, body(): pl.pallas_call(kernel, out_shape=jax.ShapeDtypeStruct(queries.shape, quer...  89.5 us

profile of v7, /device:TPU:1, one launch (start us, length us, event | category | flops | bytes accessed | tf_op | source)
XLA Modules:
  0.0 91.1 jit_solution(4828632628330358403)
XLA Ops:
  0.0 89.5 %shard_map.55 = bf16[128,1024]{1,0:T(8,128)(2,1)} custom-call(bf16[128,1024]{1,0:T(8,128)(2,1)} %q_in.1, bf16[128,1024]{1,0:T(8,128)(2,1)} %k_in.1, bf16[128,1024]{1,0:T(8,128)(2,1)} %v_in.1, s32[1,8,20]{2,1,0:T(8,128)} %lists_in.1, s32[1,8]{1,0:T(1,128)} %live_in.1), custom_call_target="tpu_custom_call" | custom-call | tf_op jit(solution)/shard_map/pallas_call | solution.py:335
  89.5 1.7 %copy.7 = bf16[128,1024]{1,0:T(8,128)(2,1)} copy(bf16[128,1024]{1,0:T(8,128)(2,1)} %shard_map.55) | data formatting | bytes 524288
